TPU v7x, 32 devices: a whole 2x2x4 slice. The times are simulated.
32 devices in a mesh: pairs: 8 (over y, x, core), fit: 4 (over z).
Axes of the slice: x: 2, y: 2, z: 4, core: 2. Of those that a mesh axis runs over, the one named last changes fastest.
Arguments:
- b_first: bfloat16 [64, 160, 3072], P('pairs', None, 'fit'), may hold values from -0.109375 to 0.109375
- b_second: bfloat16 [64, 160, 3072], P('pairs', None, 'fit'), may hold values from -6 to 6
- start_amplitudes: float32 [64, 160, 160], P('pairs'), may hold values from -1.8 to 1.8
- margins: bfloat16 [64, 96, 160, 160], P('pairs', 'fit'), may hold values from -0.5 to 0.5
- fock_terms: float32 [64, 96], P('pairs', 'fit'), may hold values from -0.2 to 0.2
- partners: int32 [64, 96], P('pairs', 'fit'), may hold values from 0 to 63, as said below
- pno_energy: float32 [64, 160], P('pairs'), may hold values from 0.3 to 1.5
- occ_energy: float32 [4000], replicated, may hold values from -1 to -0.2
- pair_list: int32 [64, 2], P('pairs'), may hold values from 0 to 3999
- pno_count: int32 [64], P('pairs'), may hold values from 64 to 160, as said below
Outputs:
- amplitudes: float32 [64, 160, 160], P('pairs')
- residual: float32 [64, 160, 160], P('pairs')
Inputs may be any that keep to these rules, and one draw needn't show every extreme that they name: `pno_count`: each pair's PNO count is one of 64, 128 and 160. `partners`: pairs owner * 8 to owner * 8 + 7 belong to one owner. In the block of one device (its 8 rows and the columns of its index along fit), each owner's pairs appear at most 48 times, and one owner's pairs appear exactly 48 times in every block.
All inputs are finite; a program needn't handle non-finite values.
Results may differ from a plain program's by a relative error of at most 0.0041.
Values may be sent and summed in bfloat16 or wider, within the bound.
A program may use at most 192 MiB of HBM per device.

v0:
```python
import jax
import jax.numpy as jnp
from jax import lax
from jax.sharding import PartitionSpec as P

ITERS = 2


def shards(
    b_first,
    b_second,
    start_amplitudes,
    margins,
    fock_terms,
    partners,
    pno_energy,
    occ_energy,
    pair_list,
    pno_count,
):
    pair_dev = start_amplitudes.shape[0]
    pno_width = pno_energy.shape[1]
    per_pair = partners.shape[1]
    request_count = pair_dev * per_pair
    levels = lax.broadcasted_iota(jnp.int32, (pair_dev, pno_width), 1)
    keep_rows = (levels < pno_count[:, None]).astype(jnp.float32)
    pair_mask = keep_rows[:, :, None] * keep_rows[:, None, :]
    occ_pair = occ_energy[pair_list[:, 0]] + occ_energy[pair_list[:, 1]]
    denominator = pno_energy[:, :, None] + pno_energy[:, None, :] - occ_pair[:, None, None]
    integral_part = jnp.einsum(
        "rap,rbp->rab", b_first, b_second, preferred_element_type=jnp.float32
    )
    flat_partners = partners.reshape(request_count)
    amplitudes = pair_mask * start_amplitudes
    residual = jnp.zeros_like(amplitudes)
    for iteration in range(ITERS):
        rounded = amplitudes.astype(jnp.bfloat16)
        everything = lax.all_gather(rounded, "pairs", axis=0, tiled=True)
        fetched = everything[flat_partners]
        fetched = fetched.reshape(pair_dev, per_pair, pno_width, pno_width)
        left_product = jnp.einsum(
            "rpac,rpcd->rpad", margins, fetched, preferred_element_type=jnp.float32
        ).astype(jnp.bfloat16)
        right_product = jnp.einsum(
            "rpad,rpbd->rpab", left_product, margins, preferred_element_type=jnp.float32
        )
        coupling = jnp.sum(fock_terms[:, :, None, None] * right_product, axis=1)
        partial_sum = integral_part - coupling
        reduced = lax.psum(partial_sum, "fit")
        residual = pair_mask * (reduced + denominator * amplitudes)
        amplitudes = amplitudes - residual / denominator
    return (amplitudes, residual)


def solution(mesh):
    return jax.shard_map(
        shards,
        mesh=mesh,
        in_specs=(
            P("pairs", None, "fit"),
            P("pairs", None, "fit"),
            P("pairs", None, None),
            P("pairs", "fit", None, None),
            P("pairs", "fit"),
            P("pairs", "fit"),
            P("pairs", None),
            P(),
            P("pairs", None),
            P("pairs"),
        ),
        out_specs=(P("pairs", None, None), P("pairs", None, None)),
        check_vma=False,
    )
```

profile of v0, /device:TPU:0, one launch (start us, length us, event | category | flops | bytes accessed | tf_op | source)
XLA Modules:
  0.0 302.0 jit_solution(12965872413875389841)
XLA Ops:
  7.2 0.0 all-gather.3.cloned.1.call-start
  7.2 0.9 fusion.15
  8.1 2.4 fusion.14
  10.5 0.0 all-gather.3.cloned.1.call-update
  10.5 0.0 all-reduce.3.cloned.1.call-start
  10.6 0.1 reshape.83
  10.7 43.7 %all-gather.3.cloned.1.call-done = bf16[64,160,160]{2,1,0:T(8,128)(2,1)} async-done(((bf16[8,160,160]{2,1,0:T(8,128)(2,1)}), bf16[64,160,160]{2,1,0:T(8,128)(2,1)}) %all-gather.3.cloned.1.call-update) | async-done | bytes 3276816 | tf_op jit(solution)/shard_map/all_gather | solution.py:38
  54.4 11.9 %gather_fusion = bf16[192,160,160]{2,1,0:T(8,128)(2,1)} fusion(bf16[64,160,160]{2,1,0:T(8,128)(2,1)} %all-gather.3.cloned.1.call-done, s32[1024]{0:T(1024)S(1)} %pad_clamp_fusion.2), kind=kCustom, calls=%fused_computation | custom fusion | bytes 19661568 | tf_op jit(solution)/shard_map/gather | solution.py:39
  66.2 21.3 %multiply_reduce_fusion.1 = f32[8,160,160]{2,1,0:T(8,128)S(1)} fusion(f32[8,24]{1,0:T(8,128)S(1)} %copy-done.8, bf16[8,24,160,160]{3,2,1,0:T(8,128)(2,1)} %param.13, bf16[8,24,160,160]{3,2,1,0:T(8,128)(2,1)} %bitcast.16), kind=kOutput, calls=%fused_computation.5 | convolution fusion | flops 3160268800 | bytes 20480768 | tf_op jit(solution)/shard_map/rpad,rpbd->rpab/dot_general | solution.py:44
  87.6 3.7 %fusion.20 = (f32[8,160,160]{2,1,0:T(8,128)}, f32[8,160,160]{2,1,0:T(8,128)}) fusion(f32[8,160,160]{2,1,0:T(8,128)S(1)} %multiply_reduce_fusion.1, bf16[8,160,768]{2,1,0:T(8,128)(2,1)S(1)} %copy-done, bf16[8,160,768]{2,1,0:T(8,128)(2,1)} %param.11), kind=kOutput, calls=%fused_computation.31 | convolution fusion | flops 314777600 | bytes 6389760 | tf_op jit(solution)/shard_map/rap,rbp->rab/dot_general | solution.py:30
  91.3 0.0 all-reduce.3.cloned.1.call-update
  91.3 0.0 all-gather.5.cloned.1.call-start
  91.4 0.6 gather_fusion.2
  92.1 0.6 gather_fusion.1
  92.7 58.8 %all-reduce.3.cloned.1.call-done = f32[8,160,160]{2,1,0:T(8,128)} async-done(((f32[8,160,160]{2,1,0:T(8,128)}), f32[8,160,160]{2,1,0:T(8,128)}) %all-reduce.3.cloned.1.call-update) | async-done | bytes 819216 | tf_op jit(solution)/shard_map/psum | solution.py:49
  151.6 2.7 fusion.18
  154.3 0.0 all-gather.5.cloned.1.call-update
  154.3 0.2 all-reduce.5.cloned.1.call-start
  154.5 40.5 %all-gather.5.cloned.1.call-done = bf16[64,160,160]{2,1,0:T(8,128)(2,1)} async-done(((bf16[8,160,160]{2,1,0:T(8,128)(2,1)}), bf16[64,160,160]{2,1,0:T(8,128)(2,1)}) %all-gather.5.cloned.1.call-update) | async-done | bytes 3276816 | tf_op jit(solution)/shard_map/all_gather | solution.py:38
  195.0 11.9 %gather_fusion.3 = bf16[192,160,160]{2,1,0:T(8,128)(2,1)} fusion(bf16[64,160,160]{2,1,0:T(8,128)(2,1)} %all-gather.5.cloned.1.call-done, s32[1024]{0:T(1024)S(1)} %pad_clamp_fusion.2), kind=kCustom, calls=%fused_computation.3 | custom fusion | bytes 19661568 | tf_op jit(solution)/shard_map/gather | solution.py:39
  206.9 22.4 %multiply_reduce_fusion = f32[8,160,160]{2,1,0:T(8,128)} fusion(f32[8,24]{1,0:T(8,128)S(1)} %copy-done.8, bf16[8,24,160,160]{3,2,1,0:T(8,128)(2,1)} %param.13, bf16[8,24,160,160]{3,2,1,0:T(8,128)(2,1)} %bitcast.15), kind=kOutput, calls=%fused_computation.4 | convolution fusion | flops 3160268800 | bytes 20480768 | tf_op jit(solution)/shard_map/rpad,rpbd->rpab/dot_general | solution.py:44
  229.3 2.5 sub.24
  231.8 60.2 %all-reduce.5.cloned.1.call-done = f32[8,160,160]{2,1,0:T(8,128)} async-done(((f32[8,160,160]{2,1,0:T(8,128)}), f32[8,160,160]{2,1,0:T(8,128)}) %all-reduce.5.cloned.1.call-update) | async-done | bytes 819216 | tf_op jit(solution)/shard_map/psum | solution.py:49
  292.1 3.4 %divide_subtract_fusion = (f32[8,160,160]{2,1,0:T(8,128)}, f32[8,160,160]{2,1,0:T(8,128)}) fusion(f32[8,160,160]{2,1,0:T(8,128)S(1)} %get-tuple-element.5, f32[8]{0:T(128)S(1)} %add.55, f32[8,160]{1,0:T(8,128)S(1)} %copy-done.5, f32[8,160,160]{2,1,0:T(8,128)} %all-reduce.5.cloned.1.call-done, f32[8,160]{1,0:T(8,128)S(1)} %fusion.15), kind=kLoop, calls=%fused_computation.17 | loop fusion | flops 1638400 | bytes 3287072 | tf_op jit(solution)/shard_map/sub | solution.py:51
  (24 shorter events, 0.1 us)
Async XLA Ops:
  7.2 80.4 %copy-start = (bf16[8,160,768]{2,1,0:T(8,128)(2,1)S(1)}, bf16[8,160,768]{2,1,0:T(8,128)(2,1)}, u32[]{:S(2)}) copy-start(bf16[8,160,768]{2,1,0:T(8,128)(2,1)} %param.10) | copy-start | bytes 5898244
  7.2 3.4 %copy-start.6 = (s32[8,24]{1,0:T(8,128)S(1)}, s32[8,24]{1,0:T(8,128)}, u32[]{:S(2)}) copy-start(s32[8,24]{1,0:T(8,128)} %param.15) | copy-start | bytes 2308
  7.2 47.2 %all-gather.3.cloned.1.call-start = ((), (), s32[]{:S(2)}) async-start(), calls=%async_computation | async-start | bytes 5898240 | tf_op jit(solution)/shard_map/all_gather | solution.py:38
  10.5 141.0 %all-reduce.3.cloned.1.call-start = ((), (), s32[]{:S(2)}) async-start(), calls=%async_computation.1 | async-start | bytes 2621440 | tf_op jit(solution)/shard_map/psum | solution.py:49
  10.7 55.6 %copy-start.8 = (f32[8,24]{1,0:T(8,128)S(1)}, f32[8,24]{1,0:T(8,128)}, u32[]{:S(2)}) copy-start(f32[8,24]{1,0:T(8,128)} %param.14) | copy-start | bytes 2308
  87.5 3.8 %copy-start.7 = (s32[8,2]{0,1:T(2,128)S(1)}, s32[8,2]{0,1:T(2,128)}, u32[]{:S(2)}) copy-start(s32[8,2]{0,1:T(2,128)} %param.18) | copy-start | bytes 196
  87.6 3.9 %copy-start.2 = (f32[4000]{0:T(1024)S(1)}, f32[4000]{0:T(1024)}, u32[]{:S(2)}) copy-start(f32[4000]{0:T(1024)} %param.17) | copy-start | bytes 48004
  91.3 60.3 %copy-start.3 = (f32[8,160,160]{2,1,0:T(8,128)S(1)}, f32[8,160,160]{2,1,0:T(8,128)}, u32[]{:S(2)}) copy-start(f32[8,160,160]{2,1,0:T(8,128)} %param.12) | copy-start | bytes 2457604
  91.3 60.3 %copy-start.5 = (f32[8,160]{1,0:T(8,128)S(1)}, f32[8,160]{1,0:T(8,128)}, u32[]{:S(2)}) copy-start(f32[8,160]{1,0:T(8,128)} %param.16) | copy-start | bytes 15364
  91.3 103.7 %all-gather.5.cloned.1.call-start = ((), (), s32[]{:S(2)}) async-start(), calls=%async_computation.2 | async-start | bytes 5898240 | tf_op jit(solution)/shard_map/all_gather | solution.py:38
  154.3 137.8 %all-reduce.5.cloned.1.call-start = ((), (), s32[]{:S(2)}) async-start(), calls=%async_computation.3 | async-start | bytes 2621440 | tf_op jit(solution)/shard_map/psum | solution.py:49
  206.9 22.4 %copy-start.4 = (f32[8,160,160]{2,1,0:T(8,128)S(1)}, f32[8,160,160]{2,1,0:T(8,128)}, u32[]{:S(2)}) copy-start(f32[8,160,160]{2,1,0:T(8,128)} %get-tuple-element.9) | copy-start | bytes 2457604
  292.1 3.4 %copy-start.1 = (bf16[8,160,768]{2,1,0:T(8,128)(2,1)S(1)}, bf16[8,160,768]{2,1,0:T(8,128)(2,1)}, u32[]{:S(2)}) copy-start(bf16[8,160,768]{2,1,0:T(8,128)(2,1)} %param.10) | copy-start | bytes 5898244
Sparse Core Ops, SparseCore 0:
  10.6 43.6 all-gather.2
  91.4 60.0 all-reduce.2
  154.4 40.5 all-gather.4
  232.0 60.0 all-reduce.4
where the time goes:
time: 302 us
  waiting for transfers between devices  203 us (67%)
  matrix products  47.4 us (16%)
  local copies, waits for them, and re-layouts  25.1 us (8%)
  between operations  13.9 us (5%)
  other arithmetic  12 us (4%)
    psum x2, waiting for transfers between devices, shards(): reduced = lax.psum(partial_sum, 'fit')  119 us
    all_gather x2, waiting for transfers between devices, shards(): everything = lax.all_gather(rounded, 'pairs', axis=0, tiled=True)  84.2 us
    dot_general x2, matrix products, shards(): jnp.einsum('rpad,rpbd->rpab', left_product, margins, preferred_element_ty...  43.7 us
    gather x2, local copies, waits for them, and re-layouts, shards(): fetched = everything[flat_partners]  23.7 us
  transfers between devices with their start and end apart: 4, of which 4 were waited for; matrix products, arithmetic and copies ran while one was open for 0% of the time, Pallas kernels for 0%

commit v1 on v0

v1 whole, which is shorter than its diff:
```python
import functools
import jax
import jax.numpy as jnp
from jax import lax
from jax.experimental import pallas as pl
from jax.experimental.pallas import tpu as pltpu
from jax.sharding import PartitionSpec as P

ITERS = 2
LANES = 128
BF16 = jnp.bfloat16
F32 = jnp.float32


def kernel(
    n_pairs,
    n_fit,
    start_ref,
    energy_ref,
    fock_ref,
    partner_ref,
    occ_ref,
    list_ref,
    count_ref,
    b_first_ref,
    b_second_ref,
    margins_ref,
    amp_out,
    res_out,
    margins,
    first,
    second,
    gathered,
    everything,
    amp_own,
    int_send,
    int_recv,
    coup_send,
    coup_recv,
    low,
    res_all,
    margin_sem,
    b_sem,
    gat_send,
    gat_fwd,
    gat_recv,
    fit_send,
    fit_recv,
    free_sem,
):
    int_own, coup_own = amp_out, res_out
    me = lax.axis_index("pairs")
    z = lax.axis_index("fit")
    chips = n_pairs // 2
    chip, core = me // 2, lax.rem(me, 2)
    sibling = chip * 2 + (1 - core)
    pair_dev, width, _ = start_ref.shape
    per_pair = margins.shape[1]
    own_pairs = pair_dev // n_fit
    tail = width - LANES
    fold = LANES // (tail * own_pairs)
    tail_rows = width // fold
    tail_at = own_pairs * width

    def margin_copy(row):
        return pltpu.make_async_copy(
            margins_ref.at[row], margins.at[row], margin_sem.at[row]
        )

    copy_first = pltpu.make_async_copy(b_first_ref, first, b_sem.at[0])
    copy_second = pltpu.make_async_copy(b_second_ref, second, b_sem.at[1])
    copy_first.start()
    copy_second.start()
    for row in range(pair_dev):
        margin_copy(row).start()

    barrier = pltpu.get_barrier_semaphore()

    def same_core(step):
        return lax.rem(chip + step, chips) * 2 + core

    def greet(sem):
        @pl.loop(1, chips)
        def _(step):
            pl.semaphore_signal(
                sem, inc=1, device_id={"pairs": same_core(step), "fit": z}
            )

        pl.semaphore_signal(sem, inc=1, device_id={"pairs": sibling, "fit": z})
        for step in range(1, n_fit):
            pl.semaphore_signal(
                sem,
                inc=1,
                device_id={"pairs": me, "fit": lax.rem(z + step, n_fit)},
            )

    greeted = chips - 1 + 1 + n_fit - 1
    greet(barrier)

    def pack(ref, blocks):
        for index, block in enumerate(blocks):
            ref[pl.ds(index * width, width), :] = block[:, :LANES].astype(ref.dtype)
        pieces = []
        for part in range(fold):
            for block in blocks:
                pieces.append(
                    block[part * tail_rows : (part + 1) * tail_rows, LANES:]
                )
        ref[pl.ds(tail_at, tail_rows), :] = jnp.concatenate(pieces, axis=1).astype(
            ref.dtype
        )

    def unpack_tail(ref, index):
        lanes = ref[pl.ds(tail_at, tail_rows), :].astype(F32)
        pieces = []
        for part in range(fold):
            at = (part * own_pairs + index) * tail
            pieces.append(lanes[:, at : at + tail])
        return jnp.concatenate(pieces, axis=0)

    def unpack(ref, index):
        main = ref[pl.ds(index * width, width), :].astype(F32)
        return jnp.concatenate([main, unpack_tail(ref, index)], axis=1)

    rows_at = lax.broadcasted_iota(jnp.int32, (width, width), 0)
    cols_at = lax.broadcasted_iota(jnp.int32, (width, width), 1)

    def mask_of(row):
        count = count_ref[row]
        keep = (rows_at < count).astype(F32) * (cols_at < count).astype(F32)
        return keep

    orbitals = lax.broadcasted_iota(jnp.int32, occ_ref.shape, 1)

    def occ_of(orbital):
        return jnp.sum(
            jnp.where(orbitals == orbital, occ_ref[...], 0.0), axis=1, keepdims=True
        )

    def denominator_of(row):
        across = jnp.broadcast_to(energy_ref[pl.ds(row, 1), :], (width, width))
        down = jnp.sum(
            jnp.where(rows_at == cols_at, across, 0.0), axis=1, keepdims=True
        )
        return down + across - (occ_of(list_ref[row, 0]) + occ_of(list_ref[row, 1]))

    @pl.loop(0, n_fit)
    def _(part):
        pack(
            gathered.at[me * n_fit + part],
            [
                mask_of(part * own_pairs + index) * start_ref[part * own_pairs + index]
                for index in range(own_pairs)
            ],
        )

    for index in range(own_pairs):
        row = z * own_pairs + index
        amp_own[index] = mask_of(row) * start_ref[row]

    pl.semaphore_wait(barrier, greeted)

    def direct(owner, part, step, target):
        slot = owner * n_fit + part
        return pltpu.make_async_remote_copy(
            src_ref=gathered.at[slot],
            dst_ref=gathered.at[slot],
            send_sem=gat_send.at[step, part],
            recv_sem=gat_recv.at[slot],
            device_id={"pairs": target, "fit": z},
        )

    def forward(owner, part):
        slot = owner * n_fit + part
        return pltpu.make_async_remote_copy(
            src_ref=gathered.at[slot],
            dst_ref=gathered.at[slot],
            send_sem=gat_fwd.at[slot],
            recv_sem=gat_recv.at[slot],
            device_id={"pairs": sibling, "fit": z},
        )

    def send_part(part):
        @pl.loop(1, chips)
        def _(step):
            direct(me, part, step, same_core(step)).start()

        forward(me, part).start()

    def fill(owner, part):
        slot = owner * n_fit + part
        for index in range(own_pairs):
            everything[slot * own_pairs + index] = unpack(
                gathered.at[slot], index
            ).astype(BF16)

    def part_at(step):
        return lax.rem(z + step, n_fit)

    def collect():
        @pl.loop(0, n_fit)
        def _(turn):
            part = part_at(turn)
            fill(me, part)

            @pl.loop(1, chips)
            def _(step):
                owner = same_core(chips - step)
                direct(owner, part, step, me).wait_recv()
                forward(owner, part).start()
                fill(owner, part)

        @pl.loop(0, n_fit)
        def _(turn):
            part = part_at(turn)

            @pl.loop(0, chips)
            def _(step):
                owner = lax.rem(chip + chips - step, chips) * 2 + (1 - core)
                forward(owner, part).wait_recv()
                fill(owner, part)

    def finish_sends():
        @pl.loop(0, n_fit)
        def _(part):
            @pl.loop(1, chips)
            def _(step):
                direct(me, part, step, same_core(step)).wait_send()
                forward(same_core(step), part).wait_send()

            forward(me, part).wait_send()

    def fit_copy(kind, step, source, target_ref):
        return pltpu.make_async_remote_copy(
            src_ref=source,
            dst_ref=target_ref,
            send_sem=fit_send.at[kind, step],
            recv_sem=fit_recv.at[kind, step],
            device_id={"pairs": me, "fit": part_at(step)},
        )

    def scatter_copy(kind, step, send, recv):
        return fit_copy(kind, step, send.at[step], recv.at[step])

    def spread_copy(kind, step, buffer, slot):
        return fit_copy(kind, step, buffer.at[slot], buffer.at[slot])

    def couple(row):
        coup_own[row] = jnp.zeros((width, width), F32)

        @pl.loop(0, per_pair // GROUP)
        def _(turn):
            total = None
            for inner in range(GROUP):
                col = turn * GROUP + inner
                partner = partner_ref[row, col]
                margin = margins[row, col]
                left = jnp.dot(
                    margin, everything[partner], preferred_element_type=F32
                ).astype(BF16)
                right = lax.dot_general(
                    left,
                    margin,
                    (((1,), (1,)), ((), ())),
                    preferred_element_type=F32,
                )
                term = fock_ref[row, col] * right
                total = term if total is None else total + term
            coup_own[row] = coup_own[row] + total

    INT, COUP, HIGH, LOW, RES = 0, 1, 3, 4, 5

    @pl.loop(0, n_fit)
    def _(part):
        send_part(part_at(part))

    copy_first.wait()
    copy_second.wait()

    def integrals_of(row):
        return lax.dot_general(
            first[row],
            second[row],
            (((1,), (1,)), ((), ())),
            preferred_element_type=F32,
        )

    @pl.loop(1, n_fit)
    def _(step):
        part = part_at(step)
        pack(
            int_send.at[step],
            [integrals_of(part * own_pairs + index) for index in range(own_pairs)],
        )
        scatter_copy(INT, step, int_send, int_recv).start()

    for index in range(own_pairs):
        int_own[index] = integrals_of(z * own_pairs + index)

    collect()

    for iteration in range(ITERS):
        if iteration == 0:
            for row in range(pair_dev):
                margin_copy(row).wait()
        sent = coup_send.at[iteration]
        got = coup_recv.at[iteration]

        @pl.loop(1, n_fit)
        def _(step):
            part = part_at(step)
            for index in range(own_pairs):
                couple(part * own_pairs + index)
            pack(
                sent.at[step],
                [coup_own[part * own_pairs + index] for index in range(own_pairs)],
            )
            scatter_copy(COUP + iteration, step, sent, got).start()

        for index in range(own_pairs):
            couple(z * own_pairs + index)

        if iteration == 0:
            finish_sends()
            greet(free_sem)

            @pl.loop(1, n_fit)
            def _(step):
                scatter_copy(INT, step, int_send, int_recv).wait()
                for index in range(own_pairs):
                    int_own[index] = int_own[index] + unpack(int_recv.at[step], index)

        @pl.loop(1, n_fit)
        def _(step):
            scatter_copy(COUP + iteration, step, sent, got).wait()
            for index in range(own_pairs):
                row = z * own_pairs + index
                coup_own[row] = coup_own[row] + unpack(got.at[step], index)

        updated, residuals = [], []
        for index in range(own_pairs):
            row = z * own_pairs + index
            denominator = denominator_of(row)
            amplitudes = amp_own[index]
            residual = mask_of(row) * (
                int_own[index] - coup_own[row] + denominator * amplitudes
            )
            residuals.append(residual)
            updated.append(amplitudes - residual / denominator)

        if iteration < ITERS - 1:
            pl.semaphore_wait(free_sem, greeted)
            mine = me * n_fit + z
            pack(gathered.at[mine], updated)
            pack(
                low.at[z],
                [block - block.astype(BF16).astype(F32) for block in updated],
            )
            for step in range(1, n_fit):
                spread_copy(HIGH, step, gathered, mine).start()
            send_part(z)
            for step in range(1, n_fit):
                spread_copy(LOW, step, low, z).start()
            for index in range(own_pairs):
                amp_own[index] = updated[index]

            @pl.loop(1, n_fit)
            def _(step):
                part = lax.rem(z + n_fit - step, n_fit)
                spread_copy(HIGH, step, gathered, me * n_fit + part).wait_recv()
                send_part(part)

            collect()
            for step in range(1, n_fit):
                spread_copy(HIGH, step, gathered, mine).wait_send()
        else:
            pack(res_all.at[z], residuals)
            for step in range(1, n_fit):
                spread_copy(RES, step, res_all, z).start()

    finish_sends()
    for step in range(1, n_fit):
        spread_copy(LOW, step, low, z).wait_send()
        part = lax.rem(z + n_fit - step, n_fit)
        spread_copy(LOW, step, low, part).wait_recv()

    @pl.loop(0, n_fit)
    def _(step):
        part = lax.rem(z + n_fit - step, n_fit)

        @pl.when(step > 0)
        def _():
            spread_copy(RES, step, res_all, part).wait_recv()

        for index in range(own_pairs):
            row = part * own_pairs + index
            residual = unpack(res_all.at[part], index)
            amplitudes = unpack(gathered.at[me * n_fit + part], index) + unpack(
                low.at[part], index
            )
            res_out[row] = residual
            amp_out[row] = amplitudes - residual / denominator_of(row)

    for step in range(1, n_fit):
        spread_copy(RES, step, res_all, z).wait_send()


GROUP = 4


def shards(
    n_pairs,
    n_fit,
    b_first,
    b_second,
    start_amplitudes,
    margins,
    fock_terms,
    partners,
    pno_energy,
    occ_energy,
    pair_list,
    pno_count,
):
    pair_dev, width, _ = start_amplitudes.shape
    own_pairs = pair_dev // n_fit
    tail = width - LANES
    packed = (own_pairs * width + own_pairs * width * tail // LANES, LANES)
    slots = n_pairs * n_fit
    out = jax.ShapeDtypeStruct(start_amplitudes.shape, F32)
    vmem = pl.BlockSpec(memory_space=pltpu.VMEM)
    smem = pl.BlockSpec(memory_space=pltpu.SMEM)
    hbm = pl.BlockSpec(memory_space=pl.ANY)
    return pl.pallas_call(
        functools.partial(kernel, n_pairs, n_fit),
        out_shape=(out, out),
        in_specs=[vmem, vmem, smem, smem, vmem, smem, smem, hbm, hbm, hbm],
        out_specs=(vmem, vmem),
        scratch_shapes=[
            pltpu.VMEM(margins.shape, BF16),
            pltpu.VMEM(b_first.shape, BF16),
            pltpu.VMEM(b_second.shape, BF16),
            pltpu.VMEM((slots,) + packed, BF16),
            pltpu.VMEM((n_pairs * pair_dev, width, width), BF16),
            pltpu.VMEM((own_pairs, width, width), F32),
            pltpu.VMEM((n_fit,) + packed, F32),
            pltpu.VMEM((n_fit,) + packed, F32),
            pltpu.VMEM((ITERS, n_fit) + packed, BF16),
            pltpu.VMEM((ITERS, n_fit) + packed, BF16),
            pltpu.VMEM((n_fit,) + packed, BF16),
            pltpu.VMEM((n_fit,) + packed, BF16),
            pltpu.SemaphoreType.DMA((pair_dev,)),
            pltpu.SemaphoreType.DMA((2,)),
            pltpu.SemaphoreType.DMA((n_pairs // 2, n_fit)),
            pltpu.SemaphoreType.DMA((slots,)),
            pltpu.SemaphoreType.DMA((slots,)),
            pltpu.SemaphoreType.DMA((6, n_fit)),
            pltpu.SemaphoreType.DMA((6, n_fit)),
            pltpu.SemaphoreType.REGULAR,
        ],
        compiler_params=pltpu.CompilerParams(
            collective_id=0, has_side_effects=True, vmem_limit_bytes=65000 * 1024
        ),
    )(
        start_amplitudes,
        pno_energy,
        fock_terms,
        partners,
        occ_energy.reshape(1, -1),
        pair_list,
        pno_count,
        b_first,
        b_second,
        margins,
    )


def solution(mesh):
    return jax.shard_map(
        functools.partial(shards, mesh.shape["pairs"], mesh.shape["fit"]),
        mesh=mesh,
        in_specs=(
            P("pairs", None, "fit"),
            P("pairs", None, "fit"),
            P("pairs", None, None),
            P("pairs", "fit", None, None),
            P("pairs", "fit"),
            P("pairs", "fit"),
            P("pairs", None),
            P(),
            P("pairs", None),
            P("pairs"),
        ),
        out_specs=(P("pairs", None, None), P("pairs", None, None)),
        check_vma=False,
    )
```

time: 302 us -> 116 us (0.38)
  waiting for transfers between devices: 203 us -> 0 us
  Pallas kernels: 0 us -> 110 us
  matrix products: 47.4 us -> 0 us
  local copies, waits for them, and re-layouts: 25.1 us -> 4.97 us
  between operations: 13.9 us -> 0.65 us
  other arithmetic: 12 us -> 0 us
    psum x2 -> x0, waiting for transfers between devices: 119 us -> none  [shards(): reduced = lax.psum(partial_sum, 'fit')]
    pallas_call x0 -> x1, Pallas kernels: none -> 110 us  [shards(): pl.pallas_call(functools.partial(kernel, n_pairs, n_fit), out_shape=(out,...]
    all_gather x2 -> x0, waiting for transfers between devices: 84.2 us -> none  [shards(): everything = lax.all_gather(rounded, 'pairs', axis=0, tiled=True)]
    dot_general x3 -> x0, matrix products: 47.4 us -> none  [the longest x2 43.7 us: shards(): jnp.einsum('rpad,rpbd->rpab', left_product, margins, preferred_element_ty...]
    gather x4 -> x0, local copies, waits for them, and re-layouts: 25 us -> none  [the longest x2 23.7 us: shards(): fetched = everything[flat_partners]]
    sub x2 -> x0, other arithmetic: 5.98 us -> none  [the longest x1 3.44 us: shards(): amplitudes = amplitudes - residual / denominator]
    convert_element_type x3 -> x0, other arithmetic: 5.95 us -> none  [the longest x2 5.1 us: shards(): rounded = amplitudes.astype(jnp.bfloat16)]
    unnamed x18 -> x5, local copies, waits for them, and re-layouts: 0.05 us -> 4.97 us
  transfers between devices with their start and end apart: 4 -> 0, of which waited for: 4 -> 0; matrix products, arithmetic and copies ran while one was open for 0% -> 0% of each run, Pallas kernels for 0% -> 0%
where the time goes in v1:
time: 116 us
  Pallas kernels  110 us (95%)
  local copies, waits for them, and re-layouts  4.97 us (4%)
    pallas_call x1, Pallas kernels, shards(): pl.pallas_call(functools.partial(kernel, n_pairs, n_fit), out_shape=(out,...  110 us
    unnamed x5, local copies, waits for them, and re-layouts  4.97 us

profile of v1, /device:TPU:0, one launch (start us, length us, event | category | flops | bytes accessed | tf_op | source)
XLA Modules:
  0.0 115.8 jit_solution(14000458912215164275)
XLA Ops:
  0.6 1.3 %copy.12.list_ref = s32[8,2]{1,0:T(8,128)} copy(s32[8,2]{0,1:T(2,128)} %param.18) | data formatting | bytes 128 | tf_op args[8]
  2.0 110.2 %shard_map.113 = (f32[8,160,160]{2,1,0:T(8,128)}, f32[8,160,160]{2,1,0:T(8,128)}) custom-call(f32[8,160,160]{2,1,0:T(8,128)} %start_ref.1, f32[8,160]{1,0:T(8,128)} %energy_ref.1, f32[8,24]{1,0:T(8,128)} %fock_ref.1, s32[8,24]{1,0:T(8,128)} %partner_ref.1, f32[1,4000]{1,0:T(1,128)} %bitcast.1, s32[8,2]{1,0:T(8,128)} %copy.12.list_ref, s32[8]{0:T(128)} %count_ref.1, ...), custom_call_target="tpu_custom_call" | custom-call | tf_op jit(solution)/shard_map/pallas_call | solution.py:434
  112.2 0.0 copy-start
  112.2 2.6 %copy.15 = f32[8,160,160]{2,1,0:T(8,128)} copy(f32[8,160,160]{2,1,0:T(8,128)} %get-tuple-element.4) | data formatting | bytes 1638400
  114.7 0.0 copy-done
  114.7 1.1 copy.16
Async XLA Ops:
  112.2 2.6 %copy-start = (f32[8,160,160]{2,1,0:T(8,128)S(1)}, f32[8,160,160]{2,1,0:T(8,128)}, u32[]{:S(2)}) copy-start(f32[8,160,160]{2,1,0:T(8,128)} %get-tuple-element.5) | copy-start | bytes 2457604

commit v2 on v1

--- a/solution.py
+++ b/solution.py
@@ -10,6 +10,16 @@
 LANES = 128
 BF16 = jnp.bfloat16
 F32 = jnp.float32
+
+
+def flip(value, bits, size):
+    result, place = 0, 1
+    while place < size:
+        one = (value // place) % 2
+        other = (bits // place) % 2
+        result = result + place * ((one + other) % 2)
+        place *= 2
+    return result
 
 
 def kernel(
@@ -33,6 +43,7 @@
     gathered,
     everything,
     amp_own,
+    denom,
     int_send,
     int_recv,
     coup_send,
@@ -43,6 +54,7 @@
     b_sem,
     gat_send,
     gat_fwd,
+    gat_relay,
     gat_recv,
     fit_send,
     fit_recv,
@@ -79,6 +91,11 @@
     def same_core(step):
         return lax.rem(chip + step, chips) * 2 + core
 
+    def part_at(step):
+        if n_fit & (n_fit - 1):
+            return lax.rem(2 * n_fit - z - step, n_fit)
+        return flip(z, step, n_fit)
+
     def greet(sem):
         @pl.loop(1, chips)
         def _(step):
@@ -91,7 +108,7 @@
             pl.semaphore_signal(
                 sem,
                 inc=1,
-                device_id={"pairs": me, "fit": lax.rem(z + step, n_fit)},
+                device_id={"pairs": me, "fit": part_at(step)},
             )
 
     greeted = chips - 1 + 1 + n_fit - 1
@@ -142,7 +159,7 @@
         down = jnp.sum(
             jnp.where(rows_at == cols_at, across, 0.0), axis=1, keepdims=True
         )
-        return down + across - (occ_of(list_ref[row, 0]) + occ_of(list_ref[row, 1]))
+        return down + across - (occ_of(list_ref[0, row]) + occ_of(list_ref[1, row]))
 
     @pl.loop(0, n_fit)
     def _(part):
@@ -180,10 +197,31 @@
             device_id={"pairs": sibling, "fit": z},
         )
 
+    relayed = chips == 4
+    near = (1, 2) if relayed else ()
+
+    def at_chip(step):
+        return flip(chip, step, chips) * 2 + core
+
+    def relay(owner, part, step):
+        slot = owner * n_fit + part
+        return pltpu.make_async_remote_copy(
+            src_ref=gathered.at[slot],
+            dst_ref=gathered.at[slot],
+            send_sem=gat_relay.at[slot],
+            recv_sem=gat_recv.at[slot],
+            device_id={"pairs": at_chip(step), "fit": z},
+        )
+
     def send_part(part):
-        @pl.loop(1, chips)
-        def _(step):
-            direct(me, part, step, same_core(step)).start()
+        if relayed:
+            for step in near:
+                direct(me, part, step, at_chip(step)).start()
+        else:
+
+            @pl.loop(1, chips)
+            def _(step):
+                direct(me, part, step, same_core(step)).start()
 
         forward(me, part).start()
 
@@ -194,13 +232,19 @@
                 gathered.at[slot], index
             ).astype(BF16)
 
-    def part_at(step):
-        return lax.rem(z + step, n_fit)
-
-    def collect():
-        @pl.loop(0, n_fit)
-        def _(turn):
-            part = part_at(turn)
+    def take_direct(turn):
+        part = part_at(turn)
+        if relayed:
+            for step in near:
+                owner = at_chip(step)
+                direct(owner, part, step, me).wait_recv()
+                if step - 1 == turn % 2:
+                    relay(owner, part, 3 - step).start()
+                forward(owner, part).start()
+            fill(me, part)
+            for step in near:
+                fill(at_chip(step), part)
+        else:
             fill(me, part)
 
             @pl.loop(1, chips)
@@ -210,6 +254,15 @@
                 forward(owner, part).start()
                 fill(owner, part)
 
+    def take_far(turn):
+        part = part_at(turn)
+        if relayed:
+            owner = at_chip(3)
+            direct(owner, part, 1, me).wait_recv()
+            forward(owner, part).start()
+            fill(owner, part)
+
+    def take_sibling():
         @pl.loop(0, n_fit)
         def _(turn):
             part = part_at(turn)
@@ -221,11 +274,20 @@
                 fill(owner, part)
 
     def finish_sends():
+        if relayed:
+            for turn in range(n_fit):
+                part = part_at(turn)
+                for step in near:
+                    direct(me, part, step, at_chip(step)).wait_send()
+                    if step - 1 == turn % 2:
+                        relay(at_chip(step), part, 3 - step).wait_send()
+
         @pl.loop(0, n_fit)
         def _(part):
             @pl.loop(1, chips)
             def _(step):
-                direct(me, part, step, same_core(step)).wait_send()
+                if not relayed:
+                    direct(me, part, step, same_core(step)).wait_send()
                 forward(same_core(step), part).wait_send()
 
             forward(me, part).wait_send()
@@ -297,7 +359,15 @@
     for index in range(own_pairs):
         int_own[index] = integrals_of(z * own_pairs + index)
 
-    collect()
+    @pl.loop(0, pair_dev)
+    def _(row):
+        denom[row] = denominator_of(row)
+
+    for turn in range(n_fit):
+        take_direct(turn)
+    for turn in range(n_fit):
+        take_far(turn)
+    take_sibling()
 
     for iteration in range(ITERS):
         if iteration == 0:
@@ -307,7 +377,8 @@
         got = coup_recv.at[iteration]
 
         @pl.loop(1, n_fit)
-        def _(step):
+        def _(turn):
+            step = n_fit - turn
             part = part_at(step)
             for index in range(own_pairs):
                 couple(part * own_pairs + index)
@@ -340,7 +411,7 @@
         updated, residuals = [], []
         for index in range(own_pairs):
             row = z * own_pairs + index
-            denominator = denominator_of(row)
+            denominator = denom[row]
             amplitudes = amp_own[index]
             residual = mask_of(row) * (
                 int_own[index] - coup_own[row] + denominator * amplitudes
@@ -364,13 +435,17 @@
             for index in range(own_pairs):
                 amp_own[index] = updated[index]
 
-            @pl.loop(1, n_fit)
-            def _(step):
-                part = lax.rem(z + n_fit - step, n_fit)
-                spread_copy(HIGH, step, gathered, me * n_fit + part).wait_recv()
+            for turn in range(1, n_fit):
+                part = part_at(turn)
+                spread_copy(HIGH, turn, gathered, me * n_fit + part).wait_recv()
                 send_part(part)
-
-            collect()
+                take_direct(turn - 1)
+                if turn > 1:
+                    take_far(turn - 2)
+            take_direct(n_fit - 1)
+            for turn in range(max(n_fit - 2, 0), n_fit):
+                take_far(turn)
+            take_sibling()
             for step in range(1, n_fit):
                 spread_copy(HIGH, step, gathered, mine).wait_send()
         else:
@@ -381,12 +456,12 @@
     finish_sends()
     for step in range(1, n_fit):
         spread_copy(LOW, step, low, z).wait_send()
-        part = lax.rem(z + n_fit - step, n_fit)
+        part = part_at(step)
         spread_copy(LOW, step, low, part).wait_recv()
 
     @pl.loop(0, n_fit)
     def _(step):
-        part = lax.rem(z + n_fit - step, n_fit)
+        part = part_at(step)
 
         @pl.when(step > 0)
         def _():
@@ -399,13 +474,13 @@
                 low.at[part], index
             )
             res_out[row] = residual
-            amp_out[row] = amplitudes - residual / denominator_of(row)
+            amp_out[row] = amplitudes - residual / denom[row]
 
     for step in range(1, n_fit):
         spread_copy(RES, step, res_all, z).wait_send()
 
 
-GROUP = 4
+GROUP = 12
 
 
 def shards(
@@ -443,6 +518,7 @@
             pltpu.VMEM((slots,) + packed, BF16),
             pltpu.VMEM((n_pairs * pair_dev, width, width), BF16),
             pltpu.VMEM((own_pairs, width, width), F32),
+            pltpu.VMEM((pair_dev, width, width), F32),
             pltpu.VMEM((n_fit,) + packed, F32),
             pltpu.VMEM((n_fit,) + packed, F32),
             pltpu.VMEM((ITERS, n_fit) + packed, BF16),
@@ -452,6 +528,7 @@
             pltpu.SemaphoreType.DMA((pair_dev,)),
             pltpu.SemaphoreType.DMA((2,)),
             pltpu.SemaphoreType.DMA((n_pairs // 2, n_fit)),
+            pltpu.SemaphoreType.DMA((slots,)),
             pltpu.SemaphoreType.DMA((slots,)),
             pltpu.SemaphoreType.DMA((slots,)),
             pltpu.SemaphoreType.DMA((6, n_fit)),
@@ -467,7 +544,7 @@
         fock_terms,
         partners,
         occ_energy.reshape(1, -1),
-        pair_list,
+        pair_list.T,
         pno_count,
         b_first,
         b_second,

time: 116 us -> 96.7 us (0.83)
  Pallas kernels: 110 us -> 92.3 us
  local copies, waits for them, and re-layouts: 4.97 us -> 3.62 us
    pallas_call x1, Pallas kernels: 110 us -> 92.3 us  [shards(): pl.pallas_call(functools.partial(kernel, n_pairs, n_fit), out_shape=(out,...]
    unnamed x5 -> x4, local copies, waits for them, and re-layouts: 4.97 us -> 3.62 us
where the time goes in v2:
time: 96.7 us; the launch traced here: 96.6 us
  Pallas kernels  92.3 us (95%)
  local copies, waits for them, and re-layouts  3.62 us (4%)
    pallas_call x1, Pallas kernels, shards(): pl.pallas_call(functools.partial(kernel, n_pairs, n_fit), out_shape=(out,...  92.3 us
    unnamed x4, local copies, waits for them, and re-layouts  3.62 us

profile of v2, /device:TPU:0, one launch (start us, length us, event | category | flops | bytes accessed | tf_op | source)
XLA Modules:
  0.0 96.6 jit_solution(2817883009238070397)
XLA Ops:
  0.6 92.3 %shard_map.113 = (f32[8,160,160]{2,1,0:T(8,128)}, f32[8,160,160]{2,1,0:T(8,128)}) custom-call(f32[8,160,160]{2,1,0:T(8,128)} %start_ref.1, f32[8,160]{1,0:T(8,128)} %energy_ref.1, f32[8,24]{1,0:T(8,128)} %fock_ref.1, s32[8,24]{1,0:T(8,128)} %partner_ref.1, f32[1,4000]{1,0:T(1,128)} %bitcast.2, s32[2,8]{1,0:T(2,128)} %bitcast.3, s32[8]{0:T(128)} %count_ref.1, ...), custom_call_target="tpu_custom_call" | custom-call | tf_op jit(solution)/shard_map/pallas_call | solution.py:509
  92.9 0.0 copy-start
  93.0 2.6 %copy.14 = f32[8,160,160]{2,1,0:T(8,128)} copy(f32[8,160,160]{2,1,0:T(8,128)} %get-tuple-element.4) | data formatting | bytes 1638400
  95.5 0.0 copy-done
  95.5 1.1 %copy.15 = f32[8,160,160]{2,1,0:T(8,128)} copy(f32[8,160,160]{2,1,0:T(8,128)S(1)} %copy-done) | data formatting | bytes 1638400
Async XLA Ops:
  92.9 2.6 %copy-start = (f32[8,160,160]{2,1,0:T(8,128)S(1)}, f32[8,160,160]{2,1,0:T(8,128)}, u32[]{:S(2)}) copy-start(f32[8,160,160]{2,1,0:T(8,128)} %get-tuple-element.5) | copy-start | bytes 2457604

commit v3 on v2

--- a/solution.py
+++ b/solution.py
@@ -430,8 +430,6 @@
             for step in range(1, n_fit):
                 spread_copy(HIGH, step, gathered, mine).start()
             send_part(z)
-            for step in range(1, n_fit):
-                spread_copy(LOW, step, low, z).start()
             for index in range(own_pairs):
                 amp_own[index] = updated[index]
 
@@ -442,6 +440,8 @@
                 take_direct(turn - 1)
                 if turn > 1:
                     take_far(turn - 2)
+            for step in range(1, n_fit):
+                spread_copy(LOW, step, low, z).start()
             take_direct(n_fit - 1)
             for turn in range(max(n_fit - 2, 0), n_fit):
                 take_far(turn)

time: 96.7 us -> 94.5 us (0.977)
  Pallas kernels: 92.3 us -> 90.1 us
    pallas_call x1, Pallas kernels: 92.3 us -> 90.1 us  [shards(): pl.pallas_call(functools.partial(kernel, n_pairs, n_fit), out_shape=(out,...]
where the time goes in v3:
time: 94.5 us; the launch traced here: 94.3 us
  Pallas kernels  90.1 us (95%)
  local copies, waits for them, and re-layouts  3.62 us (4%)
    pallas_call x1, Pallas kernels, shards(): pl.pallas_call(functools.partial(kernel, n_pairs, n_fit), out_shape=(out,...  90.1 us
    unnamed x4, local copies, waits for them, and re-layouts  3.62 us

profile of v3, /device:TPU:0, one launch (start us, length us, event | category | flops | bytes accessed | tf_op | source)
XLA Modules:
  0.0 94.3 jit_solution(16804783479165290220)
XLA Ops:
  0.6 90.1 %shard_map.113 = (f32[8,160,160]{2,1,0:T(8,128)}, f32[8,160,160]{2,1,0:T(8,128)}) custom-call(f32[8,160,160]{2,1,0:T(8,128)} %start_ref.1, f32[8,160]{1,0:T(8,128)} %energy_ref.1, f32[8,24]{1,0:T(8,128)} %fock_ref.1, s32[8,24]{1,0:T(8,128)} %partner_ref.1, f32[1,4000]{1,0:T(1,128)} %bitcast.2, s32[2,8]{1,0:T(2,128)} %bitcast.3, s32[8]{0:T(128)} %count_ref.1, ...), custom_call_target="tpu_custom_call" | custom-call | tf_op jit(solution)/shard_map/pallas_call | solution.py:509
  90.7 0.0 copy-start
  90.7 2.6 %copy.14 = f32[8,160,160]{2,1,0:T(8,128)} copy(f32[8,160,160]{2,1,0:T(8,128)} %get-tuple-element.4) | data formatting | bytes 1638400
  93.3 0.0 copy-done
  93.3 1.1 %copy.15 = f32[8,160,160]{2,1,0:T(8,128)} copy(f32[8,160,160]{2,1,0:T(8,128)S(1)} %copy-done) | data formatting | bytes 1638400
Async XLA Ops:
  90.7 2.6 %copy-start = (f32[8,160,160]{2,1,0:T(8,128)S(1)}, f32[8,160,160]{2,1,0:T(8,128)}, u32[]{:S(2)}) copy-start(f32[8,160,160]{2,1,0:T(8,128)} %get-tuple-element.5) | copy-start | bytes 2457604
